TPU v7x, 32 devices: a whole 2x2x4 slice. The times are simulated.
32 devices in a mesh: member: 2 (over x), fsdp: 16 (over z, y, core).
Axes of the slice: x: 2, y: 2, z: 4, core: 2. Of those that a mesh axis runs over, the one named last changes fastest.
Arguments:
- context: bfloat16 [4, 2048, 2048], P(None, 'fsdp', 'member'), may hold values from -6 to 6
- residual: bfloat16 [2048, 2048], P('fsdp', 'member'), may hold values from -6 to 6
- out_weight: bfloat16 [2048, 2048], P('fsdp', 'member'), may hold values from -0.1875 to 0.1875
- in_factor: bfloat16 [4, 2048], P(None, 'member'), may hold values from 0.25 to 1.75
- out_factor: bfloat16 [4, 2048], P(None, 'member'), may hold values from 0.25 to 1.75
- cotangent: bfloat16 [4, 2048, 2048], P(None, 'fsdp', 'member'), may hold values from -0.796875 to 0.796875
Outputs:
- hidden: bfloat16 [4, 2048, 2048], P(None, 'fsdp', 'member')
- grad_context: bfloat16 [4, 2048, 2048], P(None, 'fsdp', 'member')
- grad_weight: float32 [2048, 2048], P('fsdp', 'member')
- grad_in_factor: float32 [4, 2048], P(None, 'member')
- grad_out_factor: float32 [4, 2048], P(None, 'member')
- grad_residual: float32 [2048, 2048], P('fsdp', 'member')
All inputs are finite; a program needn't handle non-finite values.
Results may differ from a plain program's by a relative error of at most 0.013.
Values may be sent and summed in bfloat16 or wider, within the bound.
A program may use at most 64 MiB of HBM per device.

v0:
```python
import jax
import jax.numpy as jnp
from jax import lax
from jax.sharding import PartitionSpec as P


def per_device(context, residual, out_weight, in_factor, out_factor, cotangent):
    in_wide = in_factor.astype(jnp.float32)
    out_wide = out_factor.astype(jnp.float32)
    scaled_local = (context.astype(jnp.float32) * in_wide[:, None, :]).astype(jnp.bfloat16)
    scaled_grad = (cotangent.astype(jnp.float32) * out_wide[:, None, :]).astype(jnp.bfloat16)
    scaled_context = lax.all_gather(scaled_local, "member", axis=2, tiled=True)
    weight = lax.all_gather(out_weight, "fsdp", axis=0, tiled=True)
    projected = jnp.einsum(
        "eti,id->etd", scaled_context, weight, preferred_element_type=jnp.float32
    )
    partial_value = jnp.einsum(
        "etd,id->eti", scaled_grad, weight, preferred_element_type=jnp.float32
    )
    hidden = (residual.astype(jnp.float32)[None] + projected * out_wide[:, None, :]).astype(
        jnp.bfloat16
    )
    backward = lax.psum_scatter(
        partial_value.astype(jnp.bfloat16), "member", scatter_dimension=2, tiled=True
    ).astype(jnp.float32)
    grad_context = (backward * in_wide[:, None, :]).astype(jnp.bfloat16)
    grad_in_local = jnp.sum(context.astype(jnp.float32) * backward, axis=1)
    grad_out_local = jnp.sum(cotangent.astype(jnp.float32) * projected, axis=1)
    grad_in, grad_out = lax.psum((grad_in_local, grad_out_local), "fsdp")
    grad_block = jnp.einsum(
        "eti,etd->id", scaled_context, scaled_grad, preferred_element_type=jnp.float32
    )
    grad_weight = lax.psum_scatter(grad_block, "fsdp", scatter_dimension=0, tiled=True)
    grad_residual = jnp.sum(cotangent.astype(jnp.float32), axis=0)
    return (hidden, grad_context, grad_weight, grad_in, grad_out, grad_residual)


def solution(mesh):
    in_specs = (
        P(None, "fsdp", "member"),
        P("fsdp", "member"),
        P("fsdp", "member"),
        P(None, "member"),
        P(None, "member"),
        P(None, "fsdp", "member"),
    )
    out_specs = (
        P(None, "fsdp", "member"),
        P(None, "fsdp", "member"),
        P("fsdp", "member"),
        P(None, "member"),
        P(None, "member"),
        P("fsdp", "member"),
    )
    return jax.shard_map(
        per_device, mesh=mesh, in_specs=in_specs, out_specs=out_specs, check_vma=False
    )
```

profile of v0, /device:TPU:0, one launch (start us, length us, event | category | flops | bytes accessed | tf_op | source)
XLA Modules:
  0.0 254.6 jit_solution(12831401750798101958)
XLA Ops:
  7.2 0.0 all-gather.5.cloned.1.call-start
  7.2 0.7 all-gather.5.cloned.1.call-update
  7.9 0.0 reduce-scatter.3.cloned.1.call-start
  7.9 0.7 convert_element_type.40
  8.6 54.6 %all-gather.5.cloned.1.call-done = bf16[2048,1024]{1,0:T(8,128)(2,1)} async-done(((bf16[128,1024]{1,0:T(8,128)(2,1)}), bf16[2048,1024]{1,0:T(8,128)(2,1)}) %all-gather.5.cloned.1.call-update) | async-done | bytes 4194320 | tf_op jit(solution)/shard_map/all_gather | solution.py:13
  63.3 6.2 %fusion.4 = bf16[4,128,2048]{2,1,0:T(8,128)(2,1)} fusion(bf16[2048,1024]{1,0:T(8,128)(2,1)} %all-gather.5.cloned.1.call-done, bf16[4,128,1024]{2,1,0:T(8,128)(2,1)} %param.11, f32[4,1024]{1,0:T(4,128)S(1)} %convert_element_type.40), kind=kOutput, calls=%fused_computation.8 | convolution fusion | flops 2150105088 | bytes 7356416 | tf_op jit(solution)/shard_map/etd,id->eti/dot_general | solution.py:17
  69.5 0.0 copy-start.2
  69.5 0.0 copy-start
  69.5 0.0 reduce-scatter.3.cloned.1.call-update
  69.5 0.0 all-gather.3.cloned.1.call-start
  69.6 0.6 copy-done.2
  70.2 0.0 copy-start.4
  70.2 29.9 %reduce-scatter.3.cloned.1.call-done = bf16[4,128,1024]{2,1,0:T(8,128)(2,1)} async-done(((bf16[4,128,2048]{2,1,0:T(8,128)(2,1)}), bf16[4,128,1024]{2,1,0:T(8,128)(2,1)}) %reduce-scatter.3.cloned.1.call-update) | async-done | bytes 1048592 | tf_op jit(solution)/shard_map/reduce_scatter | solution.py:23
  100.1 0.0 copy-done
  100.1 3.2 %fusion.9 = (f32[4,1024]{1,0:T(4,128)S(1)}, bf16[4,128,1024]{2,1,0:T(8,128)(2,1)}, bf16[4,128,1024]{2,1,0:T(8,128)(2,1)}) fusion(bf16[4,128,1024]{2,1,0:T(8,128)(2,1)} %reduce-scatter.3.cloned.1.call-done, bf16[4,128,1024]{2,1,0:T(8,128)(2,1)S(1)} %copy-done, f32[4,1024]{1,0:T(4,128)S(1)} %convert_element_type.38), kind=kLoop, calls=%fused_computation.14 | loop fusion | flops 4190208 | bytes 4227072 | tf_op jit(solution)/shard_map/reduce_sum | solution.py:27
  103.3 0.0 all-gather.3.cloned.1.call-update
  103.3 0.0 reduce-scatter.5.cloned.1.call-start
  103.4 33.2 %all-gather.3.cloned.1.call-done = bf16[4,128,2048]{2,1,0:T(8,128)(2,1)} async-done(((bf16[4,128,1024]{2,1,0:T(8,128)(2,1)}), bf16[4,128,2048]{2,1,0:T(8,128)(2,1)}) %all-gather.3.cloned.1.call-update) | async-done | bytes 2097168 | tf_op jit(solution)/shard_map/all_gather | solution.py:12
  136.6 0.0 copy-done.4
  136.6 7.2 %convolution_bitcast_fusion = f32[2048,1024]{1,0:T(8,128)} fusion(bf16[4,128,2048]{2,1,0:T(8,128)(2,1)} %all-gather.3.cloned.1.call-done, bf16[4,128,1024]{2,1,0:T(8,128)(2,1)S(1)} %copy-done.4, f32[4,1024]{1,0:T(4,128)S(1)} %convert_element_type.40), kind=kOutput, calls=%fused_computation | convolution fusion | flops 2149056512 | bytes 11550720 | tf_op jit(solution)/shard_map/eti,etd->id/dot_general | solution.py:30
  143.8 0.0 copy-start.1
  143.8 0.0 copy-start.3
  143.8 0.0 reduce-scatter.5.cloned.1.call-update
  143.8 0.9 copy-done.1
  144.8 0.7 copy-done.3
  145.5 6.6 %convert_reduce_fusion = (f32[128,1024]{1,0:T(8,128)}, f32[4,1024]{1,0:T(4,128)S(1)}, bf16[4,128,1024]{2,1,0:T(8,128)(2,1)}) fusion(bf16[4,128,1024]{2,1,0:T(8,128)(2,1)S(1)} %copy-done.4, f32[4,1024]{1,0:T(4,128)S(1)} %convert_element_type.40, f32[128,1024]{1,0:T(8,128)S(1)} %convert_element_type.36, bf16[4,128,2048]{2,1,0:T(8,128)(2,1)S(1)} %copy-done.3, ...), kind=kOutput, calls=%fused_computation.5 | convolution fusion | flops 2151018496 | bytes 9469952 | tf_op jit(solution)/shard_map/eti,id->etd/dot_general | solution.py:14
  152.1 64.4 %all-reduce = (f32[4,1024]{1,0:T(4,128)}, f32[4,1024]{1,0:T(4,128)}) all-reduce(f32[4,1024]{1,0:T(4,128)S(1)} %get-tuple-element.11, f32[4,1024]{1,0:T(4,128)S(1)} %get-tuple-element.7), channel_id=1, replica_groups=mesh['member'=2,'fsdp'=16] {'fsdp'}, use_global_device_ids=true, to_apply=%region_3.0 | all-reduce | flops 8192 | bytes 65536 | tf_op jit(solution)/shard_map/psum | solution.py:29
  216.5 31.5 %reduce-scatter.5.cloned.1.call-done = f32[128,1024]{1,0:T(8,128)} async-done(((f32[2048,1024]{1,0:T(8,128)}), f32[128,1024]{1,0:T(8,128)}) %reduce-scatter.5.cloned.1.call-update) | async-done | bytes 524304 | tf_op jit(solution)/shard_map/reduce_scatter | solution.py:33
  (2 shorter events, 0.0 us)
Async XLA Ops:
  7.2 56.1 %all-gather.5.cloned.1.call-start = ((), (), s32[]{:S(2)}) async-start(), calls=%async_computation.3 | async-start | bytes 4456448 | tf_op jit(solution)/shard_map/all_gather | solution.py:13
  7.9 92.2 %reduce-scatter.3.cloned.1.call-start = ((), (), s32[]{:S(2)}) async-start(), calls=%async_computation.4 | async-start | bytes 3145728 | tf_op jit(solution)/shard_map/reduce_scatter | solution.py:23
  69.5 0.7 copy-start.2
  69.5 30.6 %copy-start = (bf16[4,128,1024]{2,1,0:T(8,128)(2,1)S(1)}, bf16[4,128,1024]{2,1,0:T(8,128)(2,1)}, u32[]{:S(2)}) copy-start(bf16[4,128,1024]{2,1,0:T(8,128)(2,1)} %param.6) | copy-start | bytes 3145732
  69.5 67.1 %all-gather.3.cloned.1.call-start = ((), (), s32[]{:S(2)}) async-start(), calls=%async_computation.2 | async-start | bytes 3145728 | tf_op jit(solution)/shard_map/all_gather | solution.py:12
  70.2 66.4 %copy-start.4 = (bf16[4,128,1024]{2,1,0:T(8,128)(2,1)S(1)}, bf16[4,128,1024]{2,1,0:T(8,128)(2,1)}, u32[]{:S(2)}) copy-start(bf16[4,128,1024]{2,1,0:T(8,128)(2,1)} %param.11) | copy-start | bytes 3145732
  103.3 144.7 %reduce-scatter.5.cloned.1.call-start = ((), (), s32[]{:S(2)}) async-start(), calls=%async_computation.5 | async-start | bytes 8912896 | tf_op jit(solution)/shard_map/reduce_scatter | solution.py:33
  143.8 0.9 copy-start.1
  143.8 1.7 copy-start.3
Sparse Core Ops, SparseCore 0:
  10.1 53.0 all-gather.4
  69.6 30.4 reduce-scatter.2
  103.5 33.0 all-gather.2
  143.9 104.0 reduce-scatter.4
where the time goes:
time: 255 us
  waiting for transfers between devices  150 us (59%)
  blocking collectives  64.4 us (25%)
  matrix products  20 us (8%)
  between operations  13.8 us (5%)
  other arithmetic  3.96 us (2%)
    psum x1, blocking collectives, per_device(): grad_in, grad_out = lax.psum((grad_in_local, grad_out_local), 'fsdp')  64.4 us
    all_gather x1, waiting for transfers between devices, per_device(): weight = lax.all_gather(out_weight, 'fsdp', axis=0, tiled=True)  54.6 us
    all_gather x1, waiting for transfers between devices, per_device(): scaled_context = lax.all_gather(scaled_local, 'member', axis=2, tiled=True)  33.2 us
    reduce_scatter x1, waiting for transfers between devices, per_device(): lax.psum_scatter(grad_block, 'fsdp', scatter_dimension=0, tiled=True)  31.5 us
    reduce_scatter x1, waiting for transfers between devices, per_device(): lax.psum_scatter(partial_value.astype(jnp.bfloat16), 'member', scatter_di...  29.9 us
    dot_general x1, matrix products, per_device(): jnp.einsum('eti,etd->id', scaled_context, scaled_grad, preferred_element_...  7.2 us
    dot_general x1, matrix products, per_device(): jnp.einsum('eti,id->etd', scaled_context, weight, preferred_element_type=...  6.61 us
    dot_general x1, matrix products, per_device(): jnp.einsum('etd,id->eti', scaled_grad, weight, preferred_element_type=jnp...  6.22 us
  transfers between devices with their start and end apart: 4, of which 4 were waited for; matrix products, arithmetic and copies ran while one was open for 3% of the time, Pallas kernels for 0%

commit v1 on v0

--- a/solution.py
+++ b/solution.py
@@ -1,10 +1,17 @@
+import functools
+
 import jax
 import jax.numpy as jnp
 from jax import lax
+from jax.experimental import pallas as pl
+from jax.experimental.pallas import tpu as pltpu
 from jax.sharding import PartitionSpec as P
 
-
-def per_device(context, residual, out_weight, in_factor, out_factor, cotangent):
+F32 = jnp.float32
+BF16 = jnp.bfloat16
+
+
+def general(context, residual, out_weight, in_factor, out_factor, cotangent):
     in_wide = in_factor.astype(jnp.float32)
     out_wide = out_factor.astype(jnp.float32)
     scaled_local = (context.astype(jnp.float32) * in_wide[:, None, :]).astype(jnp.bfloat16)
@@ -35,6 +42,310 @@
     return (hidden, grad_context, grad_weight, grad_in, grad_out, grad_residual)
 
 
+def kernel(
+    C,
+    ctx, res, w, inf, outf, cot,
+    hid, gc, gw, gi, go, gr,
+    sc, sg, wb, proj, part, xrecv, gall, psend, precv, rsend, rrecv, arb, arr,
+    cx_sem, ag_ss, ag_rs, pt_ss, pt_rs, px_ss, px_rs, ps_ss, ps_rs, rs_ss, rs_rs, ar_ss, ar_rs,
+):
+    E, T, H = ctx.shape
+    M = E * T
+    R = w.shape[0]
+    R2 = 2 * R
+    half = C // 2
+    far = C // 2
+    bits = []
+    b = 1
+    while b < 2 * C:
+        bits.append(b)
+        b *= 2
+
+    m = lax.axis_index("member")
+    f = lax.axis_index("fsdp")
+    c = f % 2
+    q = f // 2
+    p = (1 - q % 2) * (q // 2) + (q % 2) * (C - 1 - q // 2)
+
+    def chip_at(offset):
+        pos = (p + offset + C) % C
+        y = pos // half
+        return 2 * ((1 - y) * pos + y * (C - 1 - pos)) + y
+
+    peer = (1 - m, f)
+    partner = (m, q * 2 + 1 - c)
+    nxt = (m, chip_at(1) * 2 + c)
+    prv = (m, chip_at(-1) * 2 + c)
+    side = (nxt, prv)
+    sign = (1, -1)
+    flips = [(m, f + bit * (1 - 2 * ((f // bit) % 2))) for bit in bits]
+
+    def rc(src, dst, ss, rs, dev):
+        return pltpu.make_async_remote_copy(
+            src_ref=src, dst_ref=dst, send_sem=ss, recv_sem=rs,
+            device_id=dev, device_id_type=pl.DeviceIdType.MESH,
+        )
+
+    barrier = pltpu.get_barrier_semaphore()
+    greet = [peer, nxt, prv] + flips
+    for dev in greet:
+        pl.semaphore_signal(barrier, inc=1, device_id=dev, device_id_type=pl.DeviceIdType.MESH)
+
+    inw = inf[...].astype(F32)
+    outw = outf[...].astype(F32)
+    for e in range(E):
+        v = (ctx[e].astype(F32) * inw[e:e + 1]).astype(BF16)
+        for j in range(half):
+            sc[m * half + j, e * T:(e + 1) * T, :] = v[:, j * R2:(j + 1) * R2]
+
+    pl.semaphore_wait(barrier, len(greet))
+
+    def rows_of(core):
+        return pl.ds(pl.multiple_of(core * R, R), R)
+
+    cx = rc(sc.at[pl.ds(m * half, half)], sc.at[pl.ds(m * half, half)], cx_sem.at[0], cx_sem.at[1], peer)
+
+    def ag_rows(d, s):
+        if s < far:
+            return rows_of(c)
+        return pl.ds(pl.multiple_of(c * R + d * (R // 2), R // 2), R // 2)
+
+    def ag(d, s, shift):
+        qq = chip_at(-sign[d] * (s - 1 + shift))
+        dst = wb.at[qq, ag_rows(d, s)]
+        src = w if (s == 1 and shift == 0) else dst
+        return rc(src, dst, ag_ss.at[d, s - 1], ag_rs.at[d, s - 1], side[d])
+
+    def pt(k, offset, mine):
+        qq = chip_at(offset)
+        dst = wb.at[qq, rows_of(c if mine else 1 - c)]
+        src = w if (mine and k == 0) else dst
+        return rc(src, dst, pt_ss.at[k], pt_rs.at[k], partner)
+
+    sends = []
+
+    def go_send(copy):
+        copy.start()
+        sends.append(copy)
+
+    go_send(ag(0, 1, 0))
+    go_send(ag(1, 1, 0))
+    go_send(cx)
+    go_send(pt(0, 0, True))
+    wb[q, rows_of(c), :] = w[...]
+
+    for e in range(E):
+        sg[e * T:(e + 1) * T, :] = (cot[e].astype(F32) * outw[e:e + 1]).astype(BF16)
+    proj[...] = jnp.zeros(proj.shape, F32)
+
+    def px(qq):
+        return rc(part.at[qq], xrecv.at[qq % half], px_ss.at[qq % half], px_rs.at[qq % half], peer)
+
+    def ps(qq):
+        return rc(psend.at[qq], precv.at[qq], ps_ss.at[qq], ps_rs.at[qq], partner)
+
+    def gw_half(h):
+        def body(j, carry):
+            qq = h * half + j
+            g = lax.dot_general(sc[qq], sg[...], (((0,), (0,)), ((), ())), preferred_element_type=F32)
+            gall[qq, 0] = g[:R]
+            gall[qq, 1] = g[R:]
+            psend[qq] = gall[qq, 1 - c].astype(BF16)
+            ps(qq).start()
+            return carry
+        lax.fori_loop(0, half, body, 0)
+
+    def project(qq):
+        proj[...] += jnp.dot(sc[qq], wb[qq], preferred_element_type=F32)
+
+    def process(offsets):
+        def body(j, carry):
+            off = offsets[0] if len(offsets) == 1 else offsets[0] + j * (offsets[1] - offsets[0])
+            qq = chip_at(off)
+            part[qq] = lax.dot_general(
+                sg[...], wb[qq], (((1,), (1,)), ((), ())), preferred_element_type=F32
+            ).astype(BF16)
+
+            @pl.when(qq // half != m)
+            def _():
+                px(qq).start()
+
+            @pl.when(qq // half == m)
+            def _():
+                project(qq)
+            return carry
+        lax.fori_loop(0, len(offsets), body, 0)
+
+    gw_half(m)
+    pt(0, 0, False).wait_recv()
+    process([0])
+    for s in range(1, far):
+        for d in range(2):
+            ag(d, s, 1).wait_recv()
+            go_send(ag(d, s + 1, 0))
+            go_send(pt(d * (far - 1) + s, -sign[d] * s, True))
+        if s == 1:
+            gr[...] = jnp.sum(cot[...].astype(F32), axis=0)
+        for d in range(2):
+            pt(d * (far - 1) + s, -sign[d] * s, False).wait_recv()
+        process([-s, s])
+    ag(0, far, 1).wait_recv()
+    ag(1, far, 1).wait_recv()
+    go_send(pt(2 * far - 1, far, True))
+    pt(2 * far - 1, far, False).wait_recv()
+    process([far])
+
+    rc(sc.at[pl.ds((1 - m) * half, half)], sc.at[pl.ds((1 - m) * half, half)],
+       cx_sem.at[0], cx_sem.at[1], peer).wait_recv()
+    gw_half(1 - m)
+
+    def rs(d, k):
+        rows = pl.ds(d * (R // 2), R // 2) if k == 0 else pl.ds(0, R)
+        return rc(rsend.at[d, k, rows], rrecv.at[d, k, rows], rs_ss.at[d, k], rs_rs.at[d, k], side[d])
+
+    def chip_sum(qq):
+        return gall[qq, c] + precv[qq].astype(F32)
+
+    qf = chip_at(far)
+    ps(qf).wait_recv()
+    v = chip_sum(qf).astype(BF16)
+    for d in range(2):
+        lo = d * (R // 2)
+        rsend[d, 0, lo:lo + R // 2, :] = v[lo:lo + R // 2]
+        go_send(rs(d, 0))
+
+    def rs_step(k):
+        for d in range(2):
+            qq = chip_at(sign[d] * (far - k))
+            ps(qq).wait_recv()
+            v = chip_sum(qq)
+            rs(d, k - 1).wait_recv()
+            if k == 1:
+                lo = d * (R // 2)
+                other = (1 - d) * (R // 2)
+                rsend[d, k, lo:lo + R // 2, :] = (
+                    v[lo:lo + R // 2] + rrecv[d, 0, lo:lo + R // 2, :].astype(F32)
+                ).astype(BF16)
+                rsend[d, k, other:other + R // 2, :] = v[other:other + R // 2].astype(BF16)
+            else:
+                rsend[d, k] = (v + rrecv[d, k - 1].astype(F32)).astype(BF16)
+            go_send(rs(d, k))
+
+    def project_rest(lo, hi):
+        def body(j, carry):
+            project((1 - m) * half + j)
+            return carry
+        lax.fori_loop(lo, hi, body, 0)
+
+    mid = half // 2
+    project_rest(0, mid)
+    rs_step(1)
+    project_rest(mid, half)
+    rs_step(2)
+    resw = res[...].astype(F32)
+    for e in range(E):
+        pe = proj[e * T:(e + 1) * T, :]
+        hid[e] = (resw + pe * outw[e:e + 1]).astype(BF16)
+        arb[0, E + e:E + e + 1, :] = jnp.sum(cot[e].astype(F32) * pe, axis=0, keepdims=True)
+    for k in range(3, far):
+        rs_step(k)
+
+    for j in range(half):
+        qq = m * half + j
+        rc(xrecv.at[j], xrecv.at[j], px_ss.at[j], px_rs.at[j], peer).wait_recv()
+        cols = slice(j * R2, (j + 1) * R2)
+        for e in range(E):
+            rows = slice(e * T, (e + 1) * T)
+            be = part[qq, rows, :].astype(F32) + xrecv[j, rows, :].astype(F32)
+            gc[e, :, cols] = (be * inw[e:e + 1, cols]).astype(BF16)
+            arb[0, e:e + 1, cols] = jnp.sum(ctx[e, :, cols].astype(F32) * be, axis=0, keepdims=True)
+
+    def ar(i):
+        return rc(arb.at[i], arr.at[i], ar_ss.at[i], ar_rs.at[i], flips[i])
+
+    go_send(ar(0))
+    ps(q).wait_recv()
+    own = chip_sum(q)
+    rs(0, far - 1).wait_recv()
+    rs(1, far - 1).wait_recv()
+    gw[...] = own + rrecv[0, far - 1].astype(F32) + rrecv[1, far - 1].astype(F32)
+    for i in range(len(bits)):
+        ar(i).wait_recv()
+        total = arb[i] + arr[i]
+        if i + 1 < len(bits):
+            arb[i + 1] = total
+            go_send(ar(i + 1))
+        else:
+            gi[...] = total[:E]
+            go[...] = total[E:]
+
+    for copy in sends:
+        copy.wait_send()
+
+    def drain(j, carry):
+        ps(j).wait_send()
+        return carry
+    lax.fori_loop(0, C, drain, 0)
+    for j in range(half):
+        rc(part.at[(1 - m) * half + j], xrecv.at[j], px_ss.at[j], px_rs.at[j], peer).wait_send()
+
+
+def fused(C, context, residual, out_weight, in_factor, out_factor, cotangent):
+    E, T, H = context.shape
+    M = E * T
+    R = out_weight.shape[0]
+    half = C // 2
+    far = half
+    steps = (2 * C).bit_length() - 1
+    vm = pl.BlockSpec(memory_space=pltpu.VMEM)
+    dma = pltpu.SemaphoreType.DMA
+    shape = jax.ShapeDtypeStruct
+    return pl.pallas_call(
+        functools.partial(kernel, C),
+        out_shape=(
+            shape((E, T, H), BF16),
+            shape((E, T, H), BF16),
+            shape((R, H), F32),
+            shape((E, H), F32),
+            shape((E, H), F32),
+            shape((T, H), F32),
+        ),
+        in_specs=[vm] * 6,
+        out_specs=tuple([vm] * 6),
+        scratch_shapes=[
+            pltpu.VMEM((C, M, 2 * R), BF16),
+            pltpu.VMEM((M, H), BF16),
+            pltpu.VMEM((C, 2 * R, H), BF16),
+            pltpu.VMEM((M, H), F32),
+            pltpu.VMEM((C, M, 2 * R), BF16),
+            pltpu.VMEM((half, M, 2 * R), BF16),
+            pltpu.VMEM((C, 2, R, H), F32),
+            pltpu.VMEM((C, R, H), BF16),
+            pltpu.VMEM((C, R, H), BF16),
+            pltpu.VMEM((2, far, R, H), BF16),
+            pltpu.VMEM((2, far, R, H), BF16),
+            pltpu.VMEM((steps, 2 * E, H), F32),
+            pltpu.VMEM((steps, 2 * E, H), F32),
+            dma((2,)),
+            dma((2, far)),
+            dma((2, far)),
+            dma((2 * far,)),
+            dma((2 * far,)),
+            dma((half,)),
+            dma((half,)),
+            dma((C,)),
+            dma((C,)),
+            dma((2, far)),
+            dma((2, far)),
+            dma((steps,)),
+            dma((steps,)),
+        ],
+        compiler_params=pltpu.CompilerParams(
+            collective_id=0, has_side_effects=True, vmem_limit_bytes=60 * 1024 * 1024
+        ),
+    )(context, residual, out_weight, in_factor, out_factor, cotangent)
+
+
 def solution(mesh):
     in_specs = (
         P(None, "fsdp", "member"),
@@ -52,6 +363,12 @@
         P(None, "member"),
         P("fsdp", "member"),
     )
+    members = mesh.shape["member"]
+    chips = mesh.shape["fsdp"] // 2
+    if members == 2 and chips >= 8 and chips & (chips - 1) == 0:
+        per_device = functools.partial(fused, chips)
+    else:
+        per_device = general
     return jax.shard_map(
         per_device, mesh=mesh, in_specs=in_specs, out_specs=out_specs, check_vma=False
     )

time: 255 us -> 81 us (0.32)
  waiting for transfers between devices: 150 us -> 0 us
  Pallas kernels: 0 us -> 73.4 us
  blocking collectives: 64.4 us -> 0 us
  matrix products: 20 us -> 0 us
  between operations: 13.8 us -> 0.66 us
  local copies, waits for them, and re-layouts: 2.24 us -> 6.67 us
  other arithmetic: 3.96 us -> 0 us
    all_gather x2 -> x0, waiting for transfers between devices: 87.8 us -> none  [the longest x1 54.6 us: per_device(): weight = lax.all_gather(out_weight, 'fsdp', axis=0, tiled=True)]
    pallas_call x0 -> x1, Pallas kernels: none -> 73.4 us  [fused(): pl.pallas_call(functools.partial(kernel, C), out_shape=(shape((E, T, H),...]
    psum x1 -> x0, blocking collectives: 64.4 us -> none  [per_device(): grad_in, grad_out = lax.psum((grad_in_local, grad_out_local), 'fsdp')]
    reduce_scatter x2 -> x0, waiting for transfers between devices: 61.4 us -> none  [the longest x1 31.5 us: per_device(): lax.psum_scatter(grad_block, 'fsdp', scatter_dimension=0, tiled=True)]
    dot_general x3 -> x0, matrix products: 20 us -> none  [the longest x1 7.2 us: per_device(): jnp.einsum('eti,etd->id', scaled_context, scaled_grad, preferred_element_...]
    unnamed x10 -> x16, local copies, waits for them, and re-layouts: 2.24 us -> 6.67 us
    reduce_sum x1 -> x0, other arithmetic: 3.21 us -> none  [per_device(): grad_in_local = jnp.sum(context.astype(jnp.float32) * backward, axis=1)]
  transfers between devices with their start and end apart: 4 -> 0, of which waited for: 4 -> 0; matrix products, arithmetic and copies ran while one was open for 3% -> 0% of each run, Pallas kernels for 0% -> 0%
where the time goes in v1:
time: 81 us; the launch traced here: 80.7 us
  Pallas kernels  73.4 us (91%)
  local copies, waits for them, and re-layouts  6.67 us (8%)
    pallas_call x1, Pallas kernels, fused(): pl.pallas_call(functools.partial(kernel, C), out_shape=(shape((E, T, H),...  73.4 us
    unnamed x16, local copies, waits for them, and re-layouts  6.67 us

profile of v1, /device:TPU:0, one launch (start us, length us, event | category | flops | bytes accessed | tf_op | source)
XLA Modules:
  0.0 80.7 jit_solution(4211869356025626483)
XLA Ops:
  0.6 73.4 %shard_map.109 = (bf16[4,128,1024]{2,1,0:T(8,128)(2,1)}, bf16[4,128,1024]{2,1,0:T(8,128)(2,1)}, f32[128,1024]{1,0:T(8,128)}, f32[4,1024]{1,0:T(4,128)}, f32[4,1024]{1,0:T(4,128)}, /*index=5*/f32[128,1024]{1,0:T(8,128)}) custom-call(bf16[4,128,1024]{2,1,0:T(8,128)(2,1)} %ctx.1, bf16[128,1024]{1,0:T(8,128)(2,1)} %res.1, bf16[128,1024]{1,0:T(8,128)(2,1)} %w.1, ...), custom_call_target="tpu_custom_call" | custom-call | tf_op jit(solution)/shard_map/pallas_call | solution.py:303
  74.0 0.0 copy-start
  74.0 2.4 %copy.18 = bf16[4,128,1024]{2,1,0:T(8,128)(2,1)} copy(bf16[4,128,1024]{2,1,0:T(8,128)(2,1)} %get-tuple-element.12) | data formatting | bytes 2097152
  76.4 0.0 copy-done
  76.4 0.0 copy-start.2
  76.4 1.0 %copy.19 = bf16[4,128,1024]{2,1,0:T(8,128)(2,1)} copy(bf16[4,128,1024]{2,1,0:T(8,128)(2,1)S(1)} %copy-done) | data formatting | bytes 2097152
  77.4 0.4 copy-done.2
  77.8 0.0 copy-start.4
  77.8 0.0 copy-start.1
  77.8 0.8 copy.20
  78.6 0.0 copy-done.4
  78.6 0.0 copy-start.3
  78.6 0.6 copy.21
  79.2 0.1 copy-done.3
  79.3 0.6 copy.22
  79.9 0.0 copy-done.1
  79.9 0.8 copy.23
Async XLA Ops:
  74.0 2.4 %copy-start = (bf16[4,128,1024]{2,1,0:T(8,128)(2,1)S(1)}, bf16[4,128,1024]{2,1,0:T(8,128)(2,1)}, u32[]{:S(2)}) copy-start(bf16[4,128,1024]{2,1,0:T(8,128)(2,1)} %get-tuple-element.13) | copy-start | bytes 3145732
  76.4 1.4 %copy-start.2 = (f32[128,1024]{1,0:T(8,128)S(1)}, f32[128,1024]{1,0:T(8,128)}, u32[]{:S(2)}) copy-start(f32[128,1024]{1,0:T(8,128)} %get-tuple-element.14) | copy-start | bytes 1572868
  77.8 0.8 copy-start.4
  77.8 2.1 %copy-start.1 = (f32[128,1024]{1,0:T(8,128)S(1)}, f32[128,1024]{1,0:T(8,128)}, u32[]{:S(2)}) copy-start(f32[128,1024]{1,0:T(8,128)} %get-tuple-element.17) | copy-start | bytes 1572868
  78.6 0.7 copy-start.3

commit v2 on v1

--- a/solution.py
+++ b/solution.py
@@ -44,15 +44,16 @@
 
 def kernel(
     C,
-    ctx, res, w, inf, outf, cot,
+    ctx_h, res, w_h, inf, outf, cot_h,
     hid, gc, gw, gi, go, gr,
-    sc, sg, wb, proj, part, xrecv, gall, psend, precv, rsend, rrecv, arb, arr,
-    cx_sem, ag_ss, ag_rs, pt_ss, pt_rs, px_ss, px_rs, ps_ss, ps_rs, rs_ss, rs_rs, ar_ss, ar_rs,
+    ctx, cot, cbuf, infx, sc, sg, wb, proj, part, xrecv, gall, psend, precv, rsend, rrecv, arb, arr, swp,
+    ld_sem, cx_ss, cx_rs, ag_ss, ag_rs, pt_ss, pt_rs, px_ss, px_rs, ps_ss, ps_rs, rs_ss, rs_rs, ar_ss, ar_rs,
 ):
     E, T, H = ctx.shape
     M = E * T
-    R = w.shape[0]
+    R = w_h.shape[0]
     R2 = 2 * R
+    S = R // 2
     half = C // 2
     far = C // 2
     bits = []
@@ -91,49 +92,63 @@
     for dev in greet:
         pl.semaphore_signal(barrier, inc=1, device_id=dev, device_id_type=pl.DeviceIdType.MESH)
 
+    def rows_of(core):
+        return pl.ds(pl.multiple_of(core * R, R), R)
+
+    ld_ctx = pltpu.make_async_copy(ctx_h, ctx, ld_sem.at[0])
+    ld_cot = pltpu.make_async_copy(cot_h, cot, ld_sem.at[1])
+    ld_w = pltpu.make_async_copy(w_h, wb.at[q, rows_of(c)], ld_sem.at[2])
+    ld_ctx.start()
+    ld_cot.start()
+    ld_w.start()
+
     inw = inf[...].astype(F32)
     outw = outf[...].astype(F32)
+
+    def cx(e):
+        return rc(ctx_h.at[e], cbuf.at[e], cx_ss.at[e], cx_rs.at[e], peer)
+
+    cxf = rc(inf, infx, cx_ss.at[E], cx_rs.at[E], peer)
+
+    def sub(core, u):
+        return pl.ds(pl.multiple_of(core * R + u * S, S), S)
+
+    def subs(d, s):
+        return (0, 1) if s < far else (d,)
+
+    def ag(d, s, u, shift):
+        qq = chip_at(-sign[d] * (s - 1 + shift))
+        dst = wb.at[qq, sub(c, u)]
+        src = w_h.at[pl.ds(u * S, S)] if (s == 1 and shift == 0) else dst
+        return rc(src, dst, ag_ss.at[d, s - 1, u], ag_rs.at[d, s - 1, u], side[d])
+
+    def pt(k, u, offset, mine):
+        qq = chip_at(offset)
+        dst = wb.at[qq, sub(c if mine else 1 - c, u)]
+        src = w_h.at[pl.ds(u * S, S)] if (mine and k == 0) else dst
+        return rc(src, dst, pt_ss.at[k, u], pt_rs.at[k, u], partner)
+
+    sends = []
+
+    def go_send(copy):
+        copy.start()
+        sends.append(copy)
+
+    pl.semaphore_wait(barrier, len(greet))
+    go_send(cxf)
+    for e in range(E):
+        go_send(cx(e))
+    for u in range(2):
+        for d in range(2):
+            go_send(ag(d, 1, u, 0))
+        go_send(pt(0, u, 0, True))
+
+    ld_ctx.wait()
     for e in range(E):
         v = (ctx[e].astype(F32) * inw[e:e + 1]).astype(BF16)
         for j in range(half):
             sc[m * half + j, e * T:(e + 1) * T, :] = v[:, j * R2:(j + 1) * R2]
-
-    pl.semaphore_wait(barrier, len(greet))
-
-    def rows_of(core):
-        return pl.ds(pl.multiple_of(core * R, R), R)
-
-    cx = rc(sc.at[pl.ds(m * half, half)], sc.at[pl.ds(m * half, half)], cx_sem.at[0], cx_sem.at[1], peer)
-
-    def ag_rows(d, s):
-        if s < far:
-            return rows_of(c)
-        return pl.ds(pl.multiple_of(c * R + d * (R // 2), R // 2), R // 2)
-
-    def ag(d, s, shift):
-        qq = chip_at(-sign[d] * (s - 1 + shift))
-        dst = wb.at[qq, ag_rows(d, s)]
-        src = w if (s == 1 and shift == 0) else dst
-        return rc(src, dst, ag_ss.at[d, s - 1], ag_rs.at[d, s - 1], side[d])
-
-    def pt(k, offset, mine):
-        qq = chip_at(offset)
-        dst = wb.at[qq, rows_of(c if mine else 1 - c)]
-        src = w if (mine and k == 0) else dst
-        return rc(src, dst, pt_ss.at[k], pt_rs.at[k], partner)
-
-    sends = []
-
-    def go_send(copy):
-        copy.start()
-        sends.append(copy)
-
-    go_send(ag(0, 1, 0))
-    go_send(ag(1, 1, 0))
-    go_send(cx)
-    go_send(pt(0, 0, True))
-    wb[q, rows_of(c), :] = w[...]
-
+    ld_cot.wait()
     for e in range(E):
         sg[e * T:(e + 1) * T, :] = (cot[e].astype(F32) * outw[e:e + 1]).astype(BF16)
     proj[...] = jnp.zeros(proj.shape, F32)
@@ -176,60 +191,82 @@
             return carry
         lax.fori_loop(0, len(offsets), body, 0)
 
+    def rs(d, k, u):
+        rows = pl.ds(u * S, S)
+        return rc(rsend.at[d, k, rows], rrecv.at[d, k, rows], rs_ss.at[d, k, u], rs_rs.at[d, k, u], side[d])
+
+    def chip_sum(qq, u):
+        rows = slice(u * S, (u + 1) * S)
+        return gall[qq, c, rows, :] + precv[qq, rows, :].astype(F32)
+
+    def rs_step(k, h):
+        if k == 0:
+            qf = chip_at(far)
+
+            @pl.when(qf // half == h)
+            def _():
+                ps(qf).wait_recv()
+                for d in range(2):
+                    rsend[d, 0, d * S:(d + 1) * S, :] = chip_sum(qf, d).astype(BF16)
+                    rs(d, 0, d).start()
+            return
+        for d in range(2):
+            qq = chip_at(sign[d] * (far - k))
+
+            @pl.when(qq // half == h)
+            def _():
+                ps(qq).wait_recv()
+                for u in ((1 - d, d) if k == 1 else (0, 1)):
+                    rows = slice(u * S, (u + 1) * S)
+                    v = chip_sum(qq, u)
+                    if k > 1 or u == d:
+                        rs(d, k - 1, u).wait_recv()
+                        v = v + rrecv[d, k - 1, rows, :].astype(F32)
+                    rsend[d, k, rows, :] = v.astype(BF16)
+                    rs(d, k, u).start()
+
     gw_half(m)
-    pt(0, 0, False).wait_recv()
+    ld_w.wait()
+    for u in range(2):
+        pt(0, u, 0, False).wait_recv()
     process([0])
+    cxf_in = cxf
+
+    def scale_in(e):
+        cx(e).wait_recv()
+        v = (cbuf[e].astype(F32) * infx[e:e + 1, :].astype(F32)).astype(BF16)
+        for j in range(half):
+            sc[(1 - m) * half + j, e * T:(e + 1) * T, :] = v[:, j * R2:(j + 1) * R2]
+
     for s in range(1, far):
-        for d in range(2):
-            ag(d, s, 1).wait_recv()
-            go_send(ag(d, s + 1, 0))
-            go_send(pt(d * (far - 1) + s, -sign[d] * s, True))
+        for u in range(2):
+            for d in range(2):
+                ag(d, s, u, 1).wait_recv()
+                if u in subs(d, s + 1):
+                    go_send(ag(d, s + 1, u, 0))
+                go_send(pt(d * (far - 1) + s, u, -sign[d] * s, True))
         if s == 1:
             gr[...] = jnp.sum(cot[...].astype(F32), axis=0)
-        for d in range(2):
-            pt(d * (far - 1) + s, -sign[d] * s, False).wait_recv()
+        rs_step(s - 1, m)
+        for u in range(2):
+            for d in range(2):
+                pt(d * (far - 1) + s, u, -sign[d] * s, False).wait_recv()
         process([-s, s])
-    ag(0, far, 1).wait_recv()
-    ag(1, far, 1).wait_recv()
-    go_send(pt(2 * far - 1, far, True))
-    pt(2 * far - 1, far, False).wait_recv()
+        if s == 1:
+            cxf_in.wait_recv()
+        if s >= 2 and s - 2 < E:
+            scale_in(s - 2)
+    for d in range(2):
+        ag(d, far, d, 1).wait_recv()
+        go_send(pt(2 * far - 1, d, far, True))
+    for d in range(2):
+        pt(2 * far - 1, d, far, False).wait_recv()
     process([far])
-
-    rc(sc.at[pl.ds((1 - m) * half, half)], sc.at[pl.ds((1 - m) * half, half)],
-       cx_sem.at[0], cx_sem.at[1], peer).wait_recv()
+    for e in range(max(min(far - 2, E), 0), E):
+        scale_in(e)
     gw_half(1 - m)
-
-    def rs(d, k):
-        rows = pl.ds(d * (R // 2), R // 2) if k == 0 else pl.ds(0, R)
-        return rc(rsend.at[d, k, rows], rrecv.at[d, k, rows], rs_ss.at[d, k], rs_rs.at[d, k], side[d])
-
-    def chip_sum(qq):
-        return gall[qq, c] + precv[qq].astype(F32)
-
-    qf = chip_at(far)
-    ps(qf).wait_recv()
-    v = chip_sum(qf).astype(BF16)
-    for d in range(2):
-        lo = d * (R // 2)
-        rsend[d, 0, lo:lo + R // 2, :] = v[lo:lo + R // 2]
-        go_send(rs(d, 0))
-
-    def rs_step(k):
-        for d in range(2):
-            qq = chip_at(sign[d] * (far - k))
-            ps(qq).wait_recv()
-            v = chip_sum(qq)
-            rs(d, k - 1).wait_recv()
-            if k == 1:
-                lo = d * (R // 2)
-                other = (1 - d) * (R // 2)
-                rsend[d, k, lo:lo + R // 2, :] = (
-                    v[lo:lo + R // 2] + rrecv[d, 0, lo:lo + R // 2, :].astype(F32)
-                ).astype(BF16)
-                rsend[d, k, other:other + R // 2, :] = v[other:other + R // 2].astype(BF16)
-            else:
-                rsend[d, k] = (v + rrecv[d, k - 1].astype(F32)).astype(BF16)
-            go_send(rs(d, k))
+    rs_step(0, 1 - m)
+    rs_step(far - 1, m)
 
     def project_rest(lo, hi):
         def body(j, carry):
@@ -237,50 +274,77 @@
             return carry
         lax.fori_loop(lo, hi, body, 0)
 
-    mid = half // 2
-    project_rest(0, mid)
-    rs_step(1)
-    project_rest(mid, half)
-    rs_step(2)
+    project_rest(0, half)
     resw = res[...].astype(F32)
     for e in range(E):
         pe = proj[e * T:(e + 1) * T, :]
         hid[e] = (resw + pe * outw[e:e + 1]).astype(BF16)
-        arb[0, E + e:E + e + 1, :] = jnp.sum(cot[e].astype(F32) * pe, axis=0, keepdims=True)
-    for k in range(3, far):
-        rs_step(k)
-
+        arb[0, 2 * E + e:2 * E + e + 1, :] = jnp.sum(cot[e].astype(F32) * pe, axis=0, keepdims=True)
+    rs_step(1, 1 - m)
     for j in range(half):
-        qq = m * half + j
-        rc(xrecv.at[j], xrecv.at[j], px_ss.at[j], px_rs.at[j], peer).wait_recv()
         cols = slice(j * R2, (j + 1) * R2)
         for e in range(E):
             rows = slice(e * T, (e + 1) * T)
-            be = part[qq, rows, :].astype(F32) + xrecv[j, rows, :].astype(F32)
-            gc[e, :, cols] = (be * inw[e:e + 1, cols]).astype(BF16)
-            arb[0, e:e + 1, cols] = jnp.sum(ctx[e, :, cols].astype(F32) * be, axis=0, keepdims=True)
+            a = ctx[e, :, cols].astype(F32) * part[m * half + j, rows, :].astype(F32)
+            arb[0, e:e + 1, cols] = jnp.sum(a, axis=0, keepdims=True)
+            a = cbuf[e, :, cols].astype(F32) * part[(1 - m) * half + j, rows, :].astype(F32)
+            arb[0, E + e:E + e + 1, cols] = jnp.sum(a, axis=0, keepdims=True)
 
     def ar(i):
         return rc(arb.at[i], arr.at[i], ar_ss.at[i], ar_rs.at[i], flips[i])
 
-    go_send(ar(0))
-    ps(q).wait_recv()
-    own = chip_sum(q)
-    rs(0, far - 1).wait_recv()
-    rs(1, far - 1).wait_recv()
-    gw[...] = own + rrecv[0, far - 1].astype(F32) + rrecv[1, far - 1].astype(F32)
-    for i in range(len(bits)):
+    swap = rc(swp.at[0], swp.at[1], cx_ss.at[E + 1], cx_rs.at[E + 1], peer)
+
+    def ar_step(i):
         ar(i).wait_recv()
         total = arb[i] + arr[i]
         if i + 1 < len(bits):
             arb[i + 1] = total
             go_send(ar(i + 1))
         else:
+            swp[0] = total[E:2 * E]
+            go_send(swap)
             gi[...] = total[:E]
-            go[...] = total[E:]
+            go[...] = total[2 * E:]
+
+    go_send(ar(0))
+    ar_step(0)
+    done = 1
+    for k in range(2, far):
+        rs_step(k, 1 - m)
+        if done < len(bits):
+            ar_step(done)
+            done += 1
+    while done < len(bits):
+        ar_step(done)
+        done += 1
+
+    ps(q).wait_recv()
+    for u in range(2):
+        rows = slice(u * S, (u + 1) * S)
+        own = chip_sum(q, u)
+        for d in range(2):
+            rs(d, far - 1, u).wait_recv()
+            own = own + rrecv[d, far - 1, rows, :].astype(F32)
+        gw[rows, :] = own
+
+    for j in range(half):
+        rc(xrecv.at[j], xrecv.at[j], px_ss.at[j], px_rs.at[j], peer).wait_recv()
+        cols = slice(j * R2, (j + 1) * R2)
+        for e in range(E):
+            rows = slice(e * T, (e + 1) * T)
+            be = part[m * half + j, rows, :].astype(F32) + xrecv[j, rows, :].astype(F32)
+            gc[e, :, cols] = (be * inw[e:e + 1, cols]).astype(BF16)
+
+    swap.wait_recv()
+    gi[...] += swp[1]
 
     for copy in sends:
         copy.wait_send()
+    for d in range(2):
+        for k in range(far):
+            for u in ((d,) if k == 0 else (0, 1)):
+                rs(d, k, u).wait_send()
 
     def drain(j, carry):
         ps(j).wait_send()
@@ -298,6 +362,7 @@
     far = half
     steps = (2 * C).bit_length() - 1
     vm = pl.BlockSpec(memory_space=pltpu.VMEM)
+    hbm = pl.BlockSpec(memory_space=pl.ANY)
     dma = pltpu.SemaphoreType.DMA
     shape = jax.ShapeDtypeStruct
     return pl.pallas_call(
@@ -310,9 +375,13 @@
             shape((E, H), F32),
             shape((T, H), F32),
         ),
-        in_specs=[vm] * 6,
+        in_specs=[hbm, vm, hbm, vm, vm, hbm],
         out_specs=tuple([vm] * 6),
         scratch_shapes=[
+            pltpu.VMEM((E, T, H), BF16),
+            pltpu.VMEM((E, T, H), BF16),
+            pltpu.VMEM((E, T, H), BF16),
+            pltpu.VMEM((E, H), BF16),
             pltpu.VMEM((C, M, 2 * R), BF16),
             pltpu.VMEM((M, H), BF16),
             pltpu.VMEM((C, 2 * R, H), BF16),
@@ -324,19 +393,22 @@
             pltpu.VMEM((C, R, H), BF16),
             pltpu.VMEM((2, far, R, H), BF16),
             pltpu.VMEM((2, far, R, H), BF16),
-            pltpu.VMEM((steps, 2 * E, H), F32),
-            pltpu.VMEM((steps, 2 * E, H), F32),
-            dma((2,)),
-            dma((2, far)),
-            dma((2, far)),
-            dma((2 * far,)),
-            dma((2 * far,)),
+            pltpu.VMEM((steps, 3 * E, H), F32),
+            pltpu.VMEM((steps, 3 * E, H), F32),
+            pltpu.VMEM((2, E, H), F32),
+            dma((3,)),
+            dma((E + 2,)),
+            dma((E + 2,)),
+            dma((2, far, 2)),
+            dma((2, far, 2)),
+            dma((2 * far, 2)),
+            dma((2 * far, 2)),
             dma((half,)),
             dma((half,)),
             dma((C,)),
             dma((C,)),
-            dma((2, far)),
-            dma((2, far)),
+            dma((2, far, 2)),
+            dma((2, far, 2)),
             dma((steps,)),
             dma((steps,)),
         ],

time: 81 us -> 82 us (1.012)
  the two profiles are of different devices: /device:TPU:0 before, /device:TPU:4 now
where the time goes in v2:
time: 82 us; the launch traced here: 81.8 us
  Pallas kernels  74.4 us (91%)
  local copies, waits for them, and re-layouts  6.67 us (8%)
    pallas_call x1, Pallas kernels, fused(): pl.pallas_call(functools.partial(kernel, C), out_shape=(shape((E, T, H),...  74.4 us
    unnamed x16, local copies, waits for them, and re-layouts  6.67 us

profile of v2, /device:TPU:4, one launch (start us, length us, event | category | flops | bytes accessed | tf_op | source)
XLA Modules:
  0.0 81.8 jit_solution(15232249051929585960)
XLA Ops:
  0.6 74.4 %shard_map.109 = (bf16[4,128,1024]{2,1,0:T(8,128)(2,1)}, bf16[4,128,1024]{2,1,0:T(8,128)(2,1)}, f32[128,1024]{1,0:T(8,128)}, f32[4,1024]{1,0:T(4,128)}, f32[4,1024]{1,0:T(4,128)}, /*index=5*/f32[128,1024]{1,0:T(8,128)}) custom-call(bf16[4,128,1024]{2,1,0:T(8,128)(2,1)} %ctx_h.1, bf16[128,1024]{1,0:T(8,128)(2,1)} %res.1, bf16[128,1024]{1,0:T(8,128)(2,1)} %w_h.1, ...), custom_call_target="tpu_custom_call" | custom-call | tf_op jit(solution)/shard_map/pallas_call | solution.py:368
  75.1 0.0 copy-start
  75.1 2.4 %copy.18 = bf16[4,128,1024]{2,1,0:T(8,128)(2,1)} copy(bf16[4,128,1024]{2,1,0:T(8,128)(2,1)} %get-tuple-element.12) | data formatting | bytes 2097152
  77.4 0.0 copy-done
  77.4 0.0 copy-start.2
  77.4 1.0 %copy.19 = bf16[4,128,1024]{2,1,0:T(8,128)(2,1)} copy(bf16[4,128,1024]{2,1,0:T(8,128)(2,1)S(1)} %copy-done) | data formatting | bytes 2097152
  78.4 0.4 copy-done.2
  78.8 0.0 copy-start.4
  78.8 0.0 copy-start.1
  78.8 0.8 copy.20
  79.6 0.0 copy-done.4
  79.6 0.0 copy-start.3
  79.6 0.6 copy.21
  80.2 0.1 copy-done.3
  80.4 0.6 copy.22
  81.0 0.0 copy-done.1
  81.0 0.8 copy.23
Async XLA Ops:
  75.1 2.4 %copy-start = (bf16[4,128,1024]{2,1,0:T(8,128)(2,1)S(1)}, bf16[4,128,1024]{2,1,0:T(8,128)(2,1)}, u32[]{:S(2)}) copy-start(bf16[4,128,1024]{2,1,0:T(8,128)(2,1)} %get-tuple-element.13) | copy-start | bytes 3145732
  77.4 1.4 %copy-start.2 = (f32[128,1024]{1,0:T(8,128)S(1)}, f32[128,1024]{1,0:T(8,128)}, u32[]{:S(2)}) copy-start(f32[128,1024]{1,0:T(8,128)} %get-tuple-element.14) | copy-start | bytes 1572868
  78.8 0.8 copy-start.4
  78.8 2.1 %copy-start.1 = (f32[128,1024]{1,0:T(8,128)S(1)}, f32[128,1024]{1,0:T(8,128)}, u32[]{:S(2)}) copy-start(f32[128,1024]{1,0:T(8,128)} %get-tuple-element.17) | copy-start | bytes 1572868
  79.6 0.7 copy-start.3

commit v3 on v2

--- a/solution.py
+++ b/solution.py
@@ -106,9 +106,9 @@
     outw = outf[...].astype(F32)
 
     def cx(e):
-        return rc(ctx_h.at[e], cbuf.at[e], cx_ss.at[e], cx_rs.at[e], peer)
-
-    cxf = rc(inf, infx, cx_ss.at[E], cx_rs.at[E], peer)
+        return rc(ctx_h.at[:, :, pl.ds(e * R2, R2)], cbuf.at[e], cx_ss.at[e], cx_rs.at[e], peer)
+
+    cxf = rc(inf, infx, cx_ss.at[half], cx_rs.at[half], peer)
 
     def sub(core, u):
         return pl.ds(pl.multiple_of(core * R + u * S, S), S)
@@ -136,8 +136,8 @@
 
     pl.semaphore_wait(barrier, len(greet))
     go_send(cxf)
-    for e in range(E):
-        go_send(cx(e))
+    for j in range(half):
+        go_send(cx(j))
     for u in range(2):
         for d in range(2):
             go_send(ag(d, 1, u, 0))
@@ -159,14 +159,16 @@
     def ps(qq):
         return rc(psend.at[qq], precv.at[qq], ps_ss.at[qq], ps_rs.at[qq], partner)
 
+    def gw_one(qq):
+        g = lax.dot_general(sc[qq], sg[...], (((0,), (0,)), ((), ())), preferred_element_type=F32)
+        gall[qq, 0] = g[:R]
+        gall[qq, 1] = g[R:]
+        psend[qq] = gall[qq, 1 - c].astype(BF16)
+        ps(qq).start()
+
     def gw_half(h):
         def body(j, carry):
-            qq = h * half + j
-            g = lax.dot_general(sc[qq], sg[...], (((0,), (0,)), ((), ())), preferred_element_type=F32)
-            gall[qq, 0] = g[:R]
-            gall[qq, 1] = g[R:]
-            psend[qq] = gall[qq, 1 - c].astype(BF16)
-            ps(qq).start()
+            gw_one(h * half + j)
             return carry
         lax.fori_loop(0, half, body, 0)
 
@@ -199,31 +201,27 @@
         rows = slice(u * S, (u + 1) * S)
         return gall[qq, c, rows, :] + precv[qq, rows, :].astype(F32)
 
-    def rs_step(k, h):
+    def rs_step(k):
         if k == 0:
             qf = chip_at(far)
-
-            @pl.when(qf // half == h)
-            def _():
-                ps(qf).wait_recv()
-                for d in range(2):
-                    rsend[d, 0, d * S:(d + 1) * S, :] = chip_sum(qf, d).astype(BF16)
-                    rs(d, 0, d).start()
+            ps(qf).wait_recv()
+            for d in range(2):
+                rsend[d, 0, d * S:(d + 1) * S, :] = chip_sum(qf, d).astype(BF16)
+                go_send(rs(d, 0, d))
             return
+        qs = [chip_at(sign[d] * (far - k)) for d in range(2)]
         for d in range(2):
-            qq = chip_at(sign[d] * (far - k))
-
-            @pl.when(qq // half == h)
-            def _():
-                ps(qq).wait_recv()
-                for u in ((1 - d, d) if k == 1 else (0, 1)):
-                    rows = slice(u * S, (u + 1) * S)
-                    v = chip_sum(qq, u)
-                    if k > 1 or u == d:
-                        rs(d, k - 1, u).wait_recv()
-                        v = v + rrecv[d, k - 1, rows, :].astype(F32)
-                    rsend[d, k, rows, :] = v.astype(BF16)
-                    rs(d, k, u).start()
+            ps(qs[d]).wait_recv()
+        for i in range(2):
+            for d in range(2):
+                u = (1 - d if i == 0 else d) if k == 1 else i
+                rows = slice(u * S, (u + 1) * S)
+                v = chip_sum(qs[d], u)
+                if k > 1 or u == d:
+                    rs(d, k - 1, u).wait_recv()
+                    v = v + rrecv[d, k - 1, rows, :].astype(F32)
+                rsend[d, k, rows, :] = v.astype(BF16)
+                go_send(rs(d, k, u))
 
     gw_half(m)
     ld_w.wait()
@@ -232,11 +230,12 @@
     process([0])
     cxf_in = cxf
 
-    def scale_in(e):
-        cx(e).wait_recv()
-        v = (cbuf[e].astype(F32) * infx[e:e + 1, :].astype(F32)).astype(BF16)
-        for j in range(half):
-            sc[(1 - m) * half + j, e * T:(e + 1) * T, :] = v[:, j * R2:(j + 1) * R2]
+    def scale_in(j):
+        cx(j).wait_recv()
+        for e in range(E):
+            wide = infx[e:e + 1, j * R2:(j + 1) * R2].astype(F32)
+            sc[(1 - m) * half + j, e * T:(e + 1) * T, :] = (cbuf[j, e].astype(F32) * wide).astype(BF16)
+        gw_one((1 - m) * half + j)
 
     for s in range(1, far):
         for u in range(2):
@@ -247,14 +246,13 @@
                 go_send(pt(d * (far - 1) + s, u, -sign[d] * s, True))
         if s == 1:
             gr[...] = jnp.sum(cot[...].astype(F32), axis=0)
-        rs_step(s - 1, m)
         for u in range(2):
             for d in range(2):
                 pt(d * (far - 1) + s, u, -sign[d] * s, False).wait_recv()
         process([-s, s])
         if s == 1:
             cxf_in.wait_recv()
-        if s >= 2 and s - 2 < E:
+        if s >= 2:
             scale_in(s - 2)
     for d in range(2):
         ag(d, far, d, 1).wait_recv()
@@ -262,11 +260,9 @@
     for d in range(2):
         pt(2 * far - 1, d, far, False).wait_recv()
     process([far])
-    for e in range(max(min(far - 2, E), 0), E):
-        scale_in(e)
-    gw_half(1 - m)
-    rs_step(0, 1 - m)
-    rs_step(far - 1, m)
+    for j in range(far - 2, half):
+        scale_in(j)
+    rs_step(0)
 
     def project_rest(lo, hi):
         def body(j, carry):
@@ -275,25 +271,25 @@
         lax.fori_loop(lo, hi, body, 0)
 
     project_rest(0, half)
+    rs_step(1)
     resw = res[...].astype(F32)
     for e in range(E):
         pe = proj[e * T:(e + 1) * T, :]
         hid[e] = (resw + pe * outw[e:e + 1]).astype(BF16)
         arb[0, 2 * E + e:2 * E + e + 1, :] = jnp.sum(cot[e].astype(F32) * pe, axis=0, keepdims=True)
-    rs_step(1, 1 - m)
     for j in range(half):
         cols = slice(j * R2, (j + 1) * R2)
         for e in range(E):
             rows = slice(e * T, (e + 1) * T)
             a = ctx[e, :, cols].astype(F32) * part[m * half + j, rows, :].astype(F32)
             arb[0, e:e + 1, cols] = jnp.sum(a, axis=0, keepdims=True)
-            a = cbuf[e, :, cols].astype(F32) * part[(1 - m) * half + j, rows, :].astype(F32)
+            a = cbuf[j, e].astype(F32) * part[(1 - m) * half + j, rows, :].astype(F32)
             arb[0, E + e:E + e + 1, cols] = jnp.sum(a, axis=0, keepdims=True)
 
     def ar(i):
         return rc(arb.at[i], arr.at[i], ar_ss.at[i], ar_rs.at[i], flips[i])
 
-    swap = rc(swp.at[0], swp.at[1], cx_ss.at[E + 1], cx_rs.at[E + 1], peer)
+    swap = rc(swp.at[0], swp.at[1], cx_ss.at[half + 1], cx_rs.at[half + 1], peer)
 
     def ar_step(i):
         ar(i).wait_recv()
@@ -311,7 +307,7 @@
     ar_step(0)
     done = 1
     for k in range(2, far):
-        rs_step(k, 1 - m)
+        rs_step(k)
         if done < len(bits):
             ar_step(done)
             done += 1
@@ -341,10 +337,6 @@
 
     for copy in sends:
         copy.wait_send()
-    for d in range(2):
-        for k in range(far):
-            for u in ((d,) if k == 0 else (0, 1)):
-                rs(d, k, u).wait_send()
 
     def drain(j, carry):
         ps(j).wait_send()
@@ -365,7 +357,7 @@
     hbm = pl.BlockSpec(memory_space=pl.ANY)
     dma = pltpu.SemaphoreType.DMA
     shape = jax.ShapeDtypeStruct
-    return pl.pallas_call(
+    results = pl.pallas_call(
         functools.partial(kernel, C),
         out_shape=(
             shape((E, T, H), BF16),
@@ -380,7 +372,7 @@
         scratch_shapes=[
             pltpu.VMEM((E, T, H), BF16),
             pltpu.VMEM((E, T, H), BF16),
-            pltpu.VMEM((E, T, H), BF16),
+            pltpu.VMEM((half, E, T, 2 * R), BF16),
             pltpu.VMEM((E, H), BF16),
             pltpu.VMEM((C, M, 2 * R), BF16),
             pltpu.VMEM((M, H), BF16),
@@ -397,8 +389,8 @@
             pltpu.VMEM((steps, 3 * E, H), F32),
             pltpu.VMEM((2, E, H), F32),
             dma((3,)),
-            dma((E + 2,)),
-            dma((E + 2,)),
+            dma((half + 2,)),
+            dma((half + 2,)),
             dma((2, far, 2)),
             dma((2, far, 2)),
             dma((2 * far, 2)),
@@ -416,6 +408,26 @@
             collective_id=0, has_side_effects=True, vmem_limit_bytes=60 * 1024 * 1024
         ),
     )(context, residual, out_weight, in_factor, out_factor, cotangent)
+    return pl.pallas_call(
+        deliver,
+        out_shape=tuple(shape(r.shape, r.dtype) for r in results),
+        in_specs=[hbm] * 6,
+        out_specs=tuple([hbm] * 6),
+        scratch_shapes=[pltpu.VMEM(r.shape, r.dtype) for r in results] + [dma((2, 6))],
+    )(*results)
+
+
+def deliver(*refs):
+    sources, results, held, sem = refs[:6], refs[6:12], refs[12:18], refs[18]
+    loads = [pltpu.make_async_copy(sources[i], held[i], sem.at[0, i]) for i in range(6)]
+    stores = [pltpu.make_async_copy(held[i], results[i], sem.at[1, i]) for i in range(6)]
+    for copy in loads:
+        copy.start()
+    for i in range(6):
+        loads[i].wait()
+        stores[i].start()
+    for copy in stores:
+        copy.wait()
 
 
 def solution(mesh):

time: 82 us -> 67.3 us (0.82)
  the two profiles are of different devices: /device:TPU:4 before, /device:TPU:0 now
where the time goes in v3:
time: 67.3 us; the launch traced here: 67.2 us
  Pallas kernels  66.5 us (99%)
    pallas_call x1, Pallas kernels, fused(): pl.pallas_call(functools.partial(kernel, C), out_shape=(shape((E, T, H),...  63.5 us
    pallas_call x1, Pallas kernels, fused(): pl.pallas_call(deliver, out_shape=tuple((shape(r.shape, r.dtype) for r in...  3 us

profile of v3, /device:TPU:0, one launch (start us, length us, event | category | flops | bytes accessed | tf_op | source)
XLA Modules:
  0.0 67.2 jit_solution(4535669734346557222)
XLA Ops:
  0.6 63.5 %shard_map.109 = (bf16[4,128,1024]{2,1,0:T(8,128)(2,1)}, bf16[4,128,1024]{2,1,0:T(8,128)(2,1)}, f32[128,1024]{1,0:T(8,128)}, f32[4,1024]{1,0:T(4,128)}, f32[4,1024]{1,0:T(4,128)}, /*index=5*/f32[128,1024]{1,0:T(8,128)}) custom-call(bf16[4,128,1024]{2,1,0:T(8,128)(2,1)} %ctx_h.1, bf16[128,1024]{1,0:T(8,128)(2,1)} %res.1, bf16[128,1024]{1,0:T(8,128)(2,1)} %w_h.1, ...), custom_call_target="tpu_custom_call" | custom-call | tf_op jit(solution)/shard_map/pallas_call | solution.py:360
  64.2 3.0 %shard_map.110 = (bf16[4,128,1024]{2,1,0:T(8,128)(2,1)}, bf16[4,128,1024]{2,1,0:T(8,128)(2,1)}, f32[128,1024]{1,0:T(8,128)}, f32[4,1024]{1,0:T(4,128)}, f32[4,1024]{1,0:T(4,128)}, /*index=5*/f32[128,1024]{1,0:T(8,128)}) custom-call(bf16[4,128,1024]{2,1,0:T(8,128)(2,1)} %get-tuple-element.12.refs_0_, bf16[4,128,1024]{2,1,0:T(8,128)(2,1)} %get-tuple-element.13.refs_1_, ...), custom_call_target="tpu_custom_call" | custom-call | tf_op jit(solution)/shard_map/pallas_call | solution.py:411
